TPU v7x, 256 devices: a whole 4x4x8 slice. The times are simulated.
256 devices in a mesh: row: 32 (over z, y_lo, core), col: 8 (over x, y_hi).
Axes of the slice: x: 4, y: 4 (y_hi: 2, y_lo: 2; y = y_hi * 2 + y_lo), z: 8, core: 2. Of those that a mesh axis runs over, the one named last changes fastest.
Arguments:
- activations: bfloat16 [1024, 16384], P('col', 'row'), may hold values from -6 to 6
- out_grad: bfloat16 [1024, 16384], P('col', 'row'), may hold values from -2 to 2
- gate_pre: bfloat16 [1024, 8192], P('row', 'col'), may hold values from -6 to 6
- up_pre: bfloat16 [1024, 8192], P('row', 'col'), may hold values from -6 to 6
- gate_weight: bfloat16 [16384, 8192], P('row', 'col'), may hold values from -0.046875 to 0.046875
- up_weight: bfloat16 [16384, 8192], P('row', 'col'), may hold values from -0.046875 to 0.046875
- down_weight: bfloat16 [8192, 16384], P('col', 'row'), may hold values from -0.0625 to 0.0625
Outputs:
- input_grad: bfloat16 [1024, 16384], P('col', 'row')
- gate_grad: bfloat16 [16384, 8192], P('row', 'col')
- up_grad: bfloat16 [16384, 8192], P('row', 'col')
- down_grad: bfloat16 [8192, 16384], P('col', 'row')
All inputs are finite; a program needn't handle non-finite values.
Results may differ from a plain program's by a relative error of at most 0.0051.
Values may be sent and summed in bfloat16 or wider, within the bound.
A program may use at most 64 MiB of HBM per device.

v0:
```python
import jax
import jax.numpy as jnp
from jax import lax
from jax.sharding import PartitionSpec as P


def contract_rows(left, right):
    return lax.dot_general(
        left, right, (((0,), (0,)), ((), ())), preferred_element_type=jnp.float32
    )


def contract_cols(left, right):
    return lax.dot_general(
        left, right, (((1,), (1,)), ((), ())), preferred_element_type=jnp.float32
    )


def derive(hidden_grad, gate_pre, up_pre):
    gate_val = gate_pre.astype(jnp.float32)
    up_val = up_pre.astype(jnp.float32)
    gate_sig = jax.nn.sigmoid(gate_val)
    swish_val = gate_val * gate_sig
    hidden = (swish_val * up_val).astype(jnp.bfloat16)
    gate_back = (hidden_grad * up_val * gate_sig * (1.0 + gate_val * (1.0 - gate_sig))).astype(
        jnp.bfloat16
    )
    up_back = (hidden_grad * swish_val).astype(jnp.bfloat16)
    return (hidden, gate_back, up_back)


def per_device(activations, out_grad, gate_pre, up_pre, gate_weight, up_weight, down_weight):
    acts_all, grad_all = (
        lax.all_gather(activations, "col", axis=0, tiled=True),
        lax.all_gather(out_grad, "col", axis=0, tiled=True),
    )
    grad_rows = grad_all
    hidden_grad = lax.psum_scatter(
        contract_cols(grad_rows, down_weight), "row", scatter_dimension=0, tiled=True
    )
    hidden, gate_back, up_back = derive(hidden_grad, gate_pre, up_pre)
    hid_piece = lax.all_gather(hidden, "row", axis=0, tiled=True)
    gate_piece = lax.all_gather(gate_back, "row", axis=0, tiled=True)
    up_piece = lax.all_gather(up_back, "row", axis=0, tiled=True)
    grad_rows = grad_all
    down_acc = contract_rows(hid_piece, grad_rows)
    gate_acc = contract_rows(acts_all, gate_piece)
    up_acc = contract_rows(acts_all, up_piece)
    input_rows = contract_cols(gate_piece, gate_weight) + contract_cols(up_piece, up_weight)
    input_acc = input_rows
    down_acc, gate_acc, up_acc, input_acc = (down_acc, gate_acc, up_acc, input_acc)
    input_grad = lax.psum_scatter(input_acc, "col", scatter_dimension=0, tiled=True)
    return (
        input_grad.astype(jnp.bfloat16),
        gate_acc.astype(jnp.bfloat16),
        up_acc.astype(jnp.bfloat16),
        down_acc.astype(jnp.bfloat16),
    )


def solution(mesh):
    placed = (
        P("col", "row"),
        P("col", "row"),
        P("row", "col"),
        P("row", "col"),
        P("row", "col"),
        P("row", "col"),
        P("col", "row"),
    )
    return jax.shard_map(
        per_device,
        mesh=mesh,
        in_specs=placed,
        out_specs=(P("col", "row"), P("row", "col"), P("row", "col"), P("col", "row")),
        check_vma=False,
    )
```

profile of v0, /device:TPU:32, one launch (start us, length us, event | category | flops | bytes accessed | tf_op | source)
XLA Modules:
  0.0 538.8 jit_solution(6172015009212809988)
XLA Ops:
  7.2 0.0 copy-start
  7.2 0.0 all-gather.6.cloned.1.call-start
  7.2 0.7 all-gather.6.cloned.1.call-update
  7.9 0.0 reduce-scatter.3.cloned.1.call-start
  8.0 57.5 %all-gather.6.cloned.1.call-done = bf16[1024,512]{1,0:T(8,128)(2,1)} async-done(((bf16[128,512]{1,0:T(8,128)(2,1)}), bf16[1024,512]{1,0:T(8,128)(2,1)}) %all-gather.6.cloned.1.call-update) | async-done | bytes 1048592 | tf_op jit(solution)/shard_map/all_gather | solution.py:35
  65.5 0.0 copy-done
  65.5 4.4 fusion.10
  69.9 0.0 copy-start.1
  69.9 0.0 copy-start.2
  70.0 0.0 copy-start.3
  70.0 0.0 reduce-scatter.3.cloned.1.call-update
  70.0 0.0 all-gather.8.cloned.1.call-start
  70.0 117.0 %reduce-scatter.3.cloned.1.call-done = f32[32,1024]{1,0:T(8,128)} async-done(((f32[1024,1024]{1,0:T(8,128)}), f32[32,1024]{1,0:T(8,128)}) %reduce-scatter.3.cloned.1.call-update) | async-done | bytes 131088 | tf_op jit(solution)/shard_map/reduce_scatter | solution.py:38
  187.1 0.0 copy-done.1
  187.1 0.0 copy-done.2
  187.1 1.6 multiply_convert_fusion
  188.7 0.0 all-gather.8.cloned.1.call-update
  188.7 0.0 all-gather.10.cloned.1.call-start
  188.8 0.5 all-gather.10.cloned.1.call-update
  189.3 0.0 all-gather.12.cloned.1.call-start
  189.4 0.5 all-gather.12.cloned.1.call-update
  189.9 0.0 all-gather.14.cloned.1.call-start
  189.9 0.5 all-gather.14.cloned.1.call-update
  190.5 0.0 copy-start.4
  190.5 0.0 reduce-scatter.5.cloned.1.call-start
  190.5 67.7 %all-gather.8.cloned.1.call-done = bf16[1024,1024]{1,0:T(8,128)(2,1)} async-done(((bf16[32,1024]{1,0:T(8,128)(2,1)}), bf16[1024,1024]{1,0:T(8,128)(2,1)}) %all-gather.8.cloned.1.call-update) | async-done | bytes 2097168 | tf_op jit(solution)/shard_map/all_gather | solution.py:43
  258.2 0.0 copy-done.3
  258.2 4.2 fusion.11
  262.5 62.1 %all-gather.10.cloned.1.call-done = bf16[1024,1024]{1,0:T(8,128)(2,1)} async-done(((bf16[32,1024]{1,0:T(8,128)(2,1)}), bf16[1024,1024]{1,0:T(8,128)(2,1)}) %all-gather.10.cloned.1.call-update) | async-done | bytes 2097168 | tf_op jit(solution)/shard_map/all_gather | solution.py:44
  324.5 0.0 copy-done.4
  324.5 4.9 convolution_add_fusion
  329.4 0.0 reduce-scatter.5.cloned.1.call-update
  329.5 50.4 %all-gather.12.cloned.1.call-done = bf16[1024,512]{1,0:T(8,128)(2,1)} async-done(((bf16[128,512]{1,0:T(8,128)(2,1)}), bf16[1024,512]{1,0:T(8,128)(2,1)}) %all-gather.12.cloned.1.call-update) | async-done | bytes 1048592 | tf_op jit(solution)/shard_map/all_gather | solution.py:34
  379.9 3.1 fusion
  383.0 0.0 copy-start.6
  383.0 1.3 copy.11
  384.3 0.0 copy-done.6
  384.3 2.9 fusion.1
  387.2 0.0 copy-start.5
  387.2 1.3 copy.12
  388.6 55.5 %all-gather.14.cloned.1.call-done = bf16[1024,1024]{1,0:T(8,128)(2,1)} async-done(((bf16[32,1024]{1,0:T(8,128)(2,1)}), bf16[1024,1024]{1,0:T(8,128)(2,1)}) %all-gather.14.cloned.1.call-update) | async-done | bytes 2097168 | tf_op jit(solution)/shard_map/all_gather | solution.py:42
  444.0 0.0 copy-done.5
  444.0 3.8 convolution_convert_fusion
  447.9 82.5 %reduce-scatter.5.cloned.1.call-done = f32[128,512]{1,0:T(8,128)} async-done(((f32[1024,512]{1,0:T(8,128)}), f32[128,512]{1,0:T(8,128)}) %reduce-scatter.5.cloned.1.call-update) | async-done | bytes 262160 | tf_op jit(solution)/shard_map/reduce_scatter | solution.py:52
  530.4 1.6 convert_element_type.37
Async XLA Ops:
  7.2 58.3 %copy-start = (bf16[1024,512]{1,0:T(8,128)(2,1)S(1)}, bf16[1024,512]{1,0:T(8,128)(2,1)}, u32[]{:S(2)}) copy-start(bf16[1024,512]{1,0:T(8,128)(2,1)} %param.13) | copy-start | bytes 3145732
  7.2 58.3 %all-gather.6.cloned.1.call-start = ((), (), s32[]{:S(2)}) async-start(), calls=%async_computation.2 | async-start | bytes 1179648 | tf_op jit(solution)/shard_map/all_gather | solution.py:35
  7.9 179.1 %reduce-scatter.3.cloned.1.call-start = ((), (), s32[]{:S(2)}) async-start(), calls=%async_computation.3 | async-start | bytes 4325376 | tf_op jit(solution)/shard_map/reduce_scatter | solution.py:38
  69.9 117.1 %copy-start.1 = (bf16[32,1024]{1,0:T(8,128)(2,1)S(1)}, bf16[32,1024]{1,0:T(8,128)(2,1)}, u32[]{:S(2)}) copy-start(bf16[32,1024]{1,0:T(8,128)(2,1)} %param.9) | copy-start | bytes 196612
  69.9 117.1 %copy-start.2 = (bf16[32,1024]{1,0:T(8,128)(2,1)S(1)}, bf16[32,1024]{1,0:T(8,128)(2,1)}, u32[]{:S(2)}) copy-start(bf16[32,1024]{1,0:T(8,128)(2,1)} %param.10) | copy-start | bytes 196612
  70.0 188.3 %copy-start.3 = (bf16[512,1024]{1,0:T(8,128)(2,1)S(1)}, bf16[512,1024]{1,0:T(8,128)(2,1)}, u32[]{:S(2)}) copy-start(bf16[512,1024]{1,0:T(8,128)(2,1)} %param.11) | copy-start | bytes 3145732
  70.0 188.2 %all-gather.8.cloned.1.call-start = ((), (), s32[]{:S(2)}) async-start(), calls=%async_computation.4 | async-start | bytes 2162688 | tf_op jit(solution)/shard_map/all_gather | solution.py:43
  188.7 135.8 %all-gather.10.cloned.1.call-start = ((), (), s32[]{:S(2)}) async-start(), calls=%async_computation.5 | async-start | bytes 2162688 | tf_op jit(solution)/shard_map/all_gather | solution.py:44
  189.3 190.6 %all-gather.12.cloned.1.call-start = ((), (), s32[]{:S(2)}) async-start(), calls=%async_computation.7 | async-start | bytes 1179648 | tf_op jit(solution)/shard_map/all_gather | solution.py:34
  189.9 254.2 %all-gather.14.cloned.1.call-start = ((), (), s32[]{:S(2)}) async-start(), calls=%async_computation.8 | async-start | bytes 2162688 | tf_op jit(solution)/shard_map/all_gather | solution.py:42
  190.5 134.1 %copy-start.4 = (bf16[512,1024]{1,0:T(8,128)(2,1)S(1)}, bf16[512,1024]{1,0:T(8,128)(2,1)}, u32[]{:S(2)}) copy-start(bf16[512,1024]{1,0:T(8,128)(2,1)} %param.12) | copy-start | bytes 3145732
  190.5 339.9 %reduce-scatter.5.cloned.1.call-start = ((), (), s32[]{:S(2)}) async-start(), calls=%async_computation.6 | async-start | bytes 2359296 | tf_op jit(solution)/shard_map/reduce_scatter | solution.py:52
  383.0 1.3 copy-start.6
  387.2 56.8 %copy-start.5 = (bf16[1024,512]{1,0:T(8,128)(2,1)S(1)}, bf16[1024,512]{1,0:T(8,128)(2,1)}, u32[]{:S(2)}) copy-start(bf16[1024,512]{1,0:T(8,128)(2,1)} %all-gather.6.cloned.1.call-done) | copy-start | bytes 3145732
Sparse Core Ops, SparseCore 0:
  10.6 54.8 all-gather.5
  70.1 116.9 reduce-scatter.2
  189.5 68.6 all-gather.7
  260.5 63.9 all-gather.9
  327.0 52.8 all-gather.11
  381.6 62.4 all-gather.13
  448.1 82.2 reduce-scatter.4
where the time goes:
time: 539 us
  waiting for transfers between devices  495 us (92%)
  matrix products  23.4 us (4%)
  between operations  14.2 us (3%)
    reduce_scatter x1, waiting for transfers between devices, per_device(): lax.psum_scatter(contract_cols(grad_rows, down_weight), 'row', scatter_di...  117 us
    reduce_scatter x1, waiting for transfers between devices, per_device(): lax.psum_scatter(input_acc, 'col', scatter_dimension=0, tiled=True)  82.5 us
    all_gather x1, waiting for transfers between devices, per_device(): gate_piece = lax.all_gather(gate_back, 'row', axis=0, tiled=True)  67.7 us
    all_gather x1, waiting for transfers between devices, per_device(): up_piece = lax.all_gather(up_back, 'row', axis=0, tiled=True)  62.1 us
    all_gather x1, waiting for transfers between devices, per_device(): lax.all_gather(out_grad, 'col', axis=0, tiled=True)  57.5 us
    all_gather x1, waiting for transfers between devices, per_device(): hid_piece = lax.all_gather(hidden, 'row', axis=0, tiled=True)  55.5 us
    all_gather x1, waiting for transfers between devices, per_device(): lax.all_gather(activations, 'col', axis=0, tiled=True)  50.4 us
    dot_general x3, matrix products, contract_cols(): lax.dot_general(left, right, (((1,), (1,)), ((), ())), preferred_element_...  13.6 us
  transfers between devices with their start and end apart: 7, of which 7 were waited for; matrix products, arithmetic and copies ran while one was open for 4% of the time, Pallas kernels for 0%

commit v1 on v0

--- a/solution.py
+++ b/solution.py
@@ -39,7 +39,9 @@
         contract_cols(grad_rows, down_weight), "row", scatter_dimension=0, tiled=True
     )
     hidden, gate_back, up_back = derive(hidden_grad, gate_pre, up_pre)
-    hid_piece = lax.all_gather(hidden, "row", axis=0, tiled=True)
+    hid_piece = jnp.concatenate(
+        lax.all_to_all(jnp.stack([hidden] * lax.axis_size("row")), "row", 0, 0), axis=0
+    )
     gate_piece = lax.all_gather(gate_back, "row", axis=0, tiled=True)
     up_piece = lax.all_gather(up_back, "row", axis=0, tiled=True)
     grad_rows = grad_all

time: 539 us -> 488 us (0.905)
  waiting for transfers between devices: 495 us -> 426 us
  starting transfers between devices: 0.27 us -> 12.2 us
    all_gather x1 -> x0, waiting for transfers between devices: 55.5 us -> none  [per_device(): hid_piece = lax.all_gather(hidden, 'row', axis=0, tiled=True)]
    reduce_scatter x1, waiting for transfers between devices: 82.5 us -> 68.4 us  [per_device(): lax.psum_scatter(input_acc, 'col', scatter_dimension=0, tiled=True)]
    all_to_all x0 -> x1, starting transfers between devices: none -> 12 us  [per_device(): lax.all_to_all(jnp.stack([hidden] * lax.axis_size('row')), 'row', 0, 0)]
  transfers between devices with their start and end apart: 7 -> 7, of which waited for: 7 -> 6; matrix products, arithmetic and copies ran while one was open for 4% -> 6% of each run, Pallas kernels for 0% -> 0%
where the time goes in v1:
time: 488 us
  waiting for transfers between devices  426 us (87%)
  matrix products  25.9 us (5%)
  between operations  14.1 us (3%)
  starting transfers between devices  12.2 us (2%)
  local copies, waits for them, and re-layouts  6.17 us (1%)
    reduce_scatter x1, waiting for transfers between devices, per_device(): lax.psum_scatter(contract_cols(grad_rows, down_weight), 'row', scatter_di...  117 us
    all_gather x1, waiting for transfers between devices, per_device(): gate_piece = lax.all_gather(gate_back, 'row', axis=0, tiled=True)  69.3 us
    reduce_scatter x1, waiting for transfers between devices, per_device(): lax.psum_scatter(input_acc, 'col', scatter_dimension=0, tiled=True)  68.4 us
    all_gather x1, waiting for transfers between devices, per_device(): up_piece = lax.all_gather(up_back, 'row', axis=0, tiled=True)  62.1 us
    all_gather x1, waiting for transfers between devices, per_device(): lax.all_gather(out_grad, 'col', axis=0, tiled=True)  57.5 us
    all_gather x1, waiting for transfers between devices, per_device(): lax.all_gather(activations, 'col', axis=0, tiled=True)  50.1 us
    dot_general x3, matrix products, contract_cols(): lax.dot_general(left, right, (((1,), (1,)), ((), ())), preferred_element_...  14.2 us
    all_to_all x1, starting transfers between devices, per_device(): lax.all_to_all(jnp.stack([hidden] * lax.axis_size('row')), 'row', 0, 0)  12 us
  transfers between devices with their start and end apart: 7, of which 6 were waited for; matrix products, arithmetic and copies ran while one was open for 6% of the time, Pallas kernels for 0%

profile of v1, /device:TPU:32, one launch (start us, length us, event | category | flops | bytes accessed | tf_op | source)
XLA Modules:
  0.0 487.9 jit_solution(10217573537121033533)
XLA Ops:
  7.2 0.0 copy-start
  7.2 0.0 all-gather.5.cloned.1.call-start
  7.2 0.7 all-gather.5.cloned.1.call-update
  7.9 0.0 reduce-scatter.3.cloned.1.call-start
  8.0 57.5 %all-gather.5.cloned.1.call-done = bf16[1024,512]{1,0:T(8,128)(2,1)} async-done(((bf16[128,512]{1,0:T(8,128)(2,1)}), bf16[1024,512]{1,0:T(8,128)(2,1)}) %all-gather.5.cloned.1.call-update) | async-done | bytes 1048592 | tf_op jit(solution)/shard_map/all_gather | solution.py:35
  65.5 0.0 copy-done
  65.5 4.5 fusion.10
  70.0 0.0 copy-start.1
  70.0 0.0 copy-start.2
  70.0 0.0 reduce-scatter.3.cloned.1.call-update
  70.0 0.0 all-gather.7.cloned.1.call-start
  70.0 117.0 %reduce-scatter.3.cloned.1.call-done = f32[32,1024]{1,0:T(8,128)} async-done(((f32[1024,1024]{1,0:T(8,128)}), f32[32,1024]{1,0:T(8,128)}) %reduce-scatter.3.cloned.1.call-update) | async-done | bytes 131088 | tf_op jit(solution)/shard_map/reduce_scatter | solution.py:38
  187.1 0.0 copy-done.1
  187.1 0.0 copy-done.2
  187.1 1.6 multiply_convert_fusion
  188.7 0.0 all-gather.7.cloned.1.call-update
  188.7 0.0 all-gather.9.cloned.1.call-start
  188.8 0.5 all-gather.9.cloned.1.call-update
  189.3 0.0 all-gather.11.cloned.1.call-start
  189.4 0.5 all-gather.11.cloned.1.call-update
  189.9 1.6 stack.2
  191.5 12.0 %all-to-all-start = ((bf16[32,32,1024]{2,1,0:T(8,128)(2,1)}), bf16[32,32,1024]{2,1,0:T(8,128)(2,1)S(1)}, u32[]{:S(2)}, u32[]{:S(2)}) async-start(bf16[32,32,1024]{2,1,0:T(8,128)(2,1)} %stack.2), calls=%async_computation.2 | async-start | bytes 4194304 | tf_op jit(solution)/shard_map/all_to_all | solution.py:43
  203.5 0.0 reduce-scatter.5.cloned.1.call-start
  203.6 69.3 %all-gather.7.cloned.1.call-done = bf16[1024,1024]{1,0:T(8,128)(2,1)} async-done(((bf16[32,1024]{1,0:T(8,128)(2,1)}), bf16[1024,1024]{1,0:T(8,128)(2,1)}) %all-gather.7.cloned.1.call-update) | async-done | bytes 2097168 | tf_op jit(solution)/shard_map/all_gather | solution.py:45
  272.9 4.5 fusion.11
  277.4 62.1 %all-gather.9.cloned.1.call-done = bf16[1024,1024]{1,0:T(8,128)(2,1)} async-done(((bf16[32,1024]{1,0:T(8,128)(2,1)}), bf16[1024,1024]{1,0:T(8,128)(2,1)}) %all-gather.9.cloned.1.call-update) | async-done | bytes 2097168 | tf_op jit(solution)/shard_map/all_gather | solution.py:46
  339.5 5.2 %convolution_add_fusion = f32[1024,512]{1,0:T(8,128)} fusion(f32[1024,512]{1,0:T(8,128)} %fusion.11, bf16[1024,1024]{1,0:T(8,128)(2,1)} %all-gather.9.cloned.1.call-done, bf16[512,1024]{1,0:T(8,128)(2,1)} %param.12), kind=kOutput, calls=%fused_computation | convolution fusion | flops 1074266112 | bytes 7340032 | tf_op jit(solution)/shard_map/dot_general | solution.py:14
  344.7 0.0 reduce-scatter.5.cloned.1.call-update
  344.7 50.1 %all-gather.11.cloned.1.call-done = bf16[1024,512]{1,0:T(8,128)(2,1)} async-done(((bf16[128,512]{1,0:T(8,128)(2,1)}), bf16[1024,512]{1,0:T(8,128)(2,1)}) %all-gather.11.cloned.1.call-update) | async-done | bytes 1048592 | tf_op jit(solution)/shard_map/all_gather | solution.py:34
  394.8 4.1 fusion
  398.9 2.3 copy.11
  401.2 4.1 fusion.1
  405.3 2.3 copy.12
  407.5 0.0 all-to-all-done
  407.6 3.5 convolution_convert_fusion
  411.0 68.4 %reduce-scatter.5.cloned.1.call-done = f32[128,512]{1,0:T(8,128)} async-done(((f32[1024,512]{1,0:T(8,128)}), f32[128,512]{1,0:T(8,128)}) %reduce-scatter.5.cloned.1.call-update) | async-done | bytes 262160 | tf_op jit(solution)/shard_map/reduce_scatter | solution.py:54
  479.4 1.6 convert_element_type.37
Async XLA Ops:
  7.2 58.3 %copy-start = (bf16[1024,512]{1,0:T(8,128)(2,1)S(1)}, bf16[1024,512]{1,0:T(8,128)(2,1)}, u32[]{:S(2)}) copy-start(bf16[1024,512]{1,0:T(8,128)(2,1)} %param.13) | copy-start | bytes 3145732
  7.2 58.3 %all-gather.5.cloned.1.call-start = ((), (), s32[]{:S(2)}) async-start(), calls=%async_computation.3 | async-start | bytes 1179648 | tf_op jit(solution)/shard_map/all_gather | solution.py:35
  7.9 179.2 %reduce-scatter.3.cloned.1.call-start = ((), (), s32[]{:S(2)}) async-start(), calls=%async_computation.4 | async-start | bytes 4325376 | tf_op jit(solution)/shard_map/reduce_scatter | solution.py:38
  70.0 117.1 %copy-start.1 = (bf16[32,1024]{1,0:T(8,128)(2,1)S(1)}, bf16[32,1024]{1,0:T(8,128)(2,1)}, u32[]{:S(2)}) copy-start(bf16[32,1024]{1,0:T(8,128)(2,1)} %param.9) | copy-start | bytes 196612
  70.0 117.1 %copy-start.2 = (bf16[32,1024]{1,0:T(8,128)(2,1)S(1)}, bf16[32,1024]{1,0:T(8,128)(2,1)}, u32[]{:S(2)}) copy-start(bf16[32,1024]{1,0:T(8,128)(2,1)} %param.10) | copy-start | bytes 196612
  70.0 202.9 %all-gather.7.cloned.1.call-start = ((), (), s32[]{:S(2)}) async-start(), calls=%async_computation.5 | async-start | bytes 2162688 | tf_op jit(solution)/shard_map/all_gather | solution.py:45
  188.7 150.7 %all-gather.9.cloned.1.call-start = ((), (), s32[]{:S(2)}) async-start(), calls=%async_computation.6 | async-start | bytes 2162688 | tf_op jit(solution)/shard_map/all_gather | solution.py:46
  189.3 205.5 %all-gather.11.cloned.1.call-start = ((), (), s32[]{:S(2)}) async-start(), calls=%async_computation.8 | async-start | bytes 1179648 | tf_op jit(solution)/shard_map/all_gather | solution.py:34
  191.5 216.0 %all-to-all-start = ((bf16[32,32,1024]{2,1,0:T(8,128)(2,1)}), bf16[32,32,1024]{2,1,0:T(8,128)(2,1)S(1)}, u32[]{:S(2)}, u32[]{:S(2)}) async-start(bf16[32,32,1024]{2,1,0:T(8,128)(2,1)} %stack.2), calls=%async_computation.2 | async-start | bytes 4194304 | tf_op jit(solution)/shard_map/all_to_all | solution.py:43
  203.5 275.9 %reduce-scatter.5.cloned.1.call-start = ((), (), s32[]{:S(2)}) async-start(), calls=%async_computation.7 | async-start | bytes 2359296 | tf_op jit(solution)/shard_map/reduce_scatter | solution.py:54
Sparse Core Ops, SparseCore 0:
  10.6 54.8 all-gather.4
  70.1 116.9 reduce-scatter.2
  189.5 83.3 all-gather.6
  275.2 64.2 all-gather.8
  341.9 52.8 all-gather.10
  398.7 80.6 reduce-scatter.4
